TPU v7x, 32 devices: a whole 2x2x4 slice. The times are simulated.
32 devices in a mesh: wide: 8 (over z, core), col: 4 (over y, x).
Axes of the slice: x: 2, y: 2, z: 4, core: 2. Of those that a mesh axis runs over, the one named last changes fastest.
Arguments:
- amplitudes: float32 [2048, 2048], P('wide', 'col'), may hold values from -6 to 6
- integrals: float32 [2048, 2048], P('wide', 'col'), may hold values from -0.125 to 0.125
Outputs:
- ladder: float32 [2048, 2048], P(('wide', 'col'))
All inputs are finite; a program needn't handle non-finite values.
Results may differ from a plain program's by a relative error of at most 0.00007.
Values sent between devices are 32-bit elements; how exact they have to be, the bound alone decides.
A program may use at most 64 MiB of HBM per device.

v0:
```python
import jax
import jax.numpy as jnp
from jax import lax
from jax.sharding import PartitionSpec as P


def on_device(amplitudes, integrals):
    panel = lax.all_gather(integrals, "wide", axis=0, tiled=True)
    part = lax.dot_general(
        amplitudes,
        panel,
        (((1,), (1,)), ((), ())),
        precision=lax.Precision.HIGHEST,
        preferred_element_type=jnp.float32,
    )
    return lax.psum_scatter(part, "col", scatter_dimension=0, tiled=True)


def solution(mesh):
    return jax.shard_map(
        on_device,
        mesh=mesh,
        in_specs=(P("wide", "col"), P("wide", "col")),
        out_specs=P(("wide", "col"), None),
        check_vma=False,
    )
```

profile of v0, /device:TPU:0, one launch (start us, length us, event | category | flops | bytes accessed | tf_op | source)
XLA Modules:
  0.0 106.9 jit_solution(4373981538191259689)
XLA Ops:
  6.5 0.0 copy-start
  6.5 0.0 all-gather.2.cloned.1.call-start
  6.5 0.7 all-gather.2.cloned.1.call-update
  7.3 0.0 reduce-scatter.2.cloned.1.call-start
  7.3 51.5 %all-gather.2.cloned.1.call-done = f32[2048,512]{1,0:T(8,128)} async-done(((f32[256,512]{1,0:T(8,128)}), f32[2048,512]{1,0:T(8,128)}) %all-gather.2.cloned.1.call-update) | async-done | bytes 4194320 | tf_op jit(solution)/shard_map/all_gather | solution.py:8
  58.8 0.0 copy-done
  58.8 7.1 %fusion = f32[256,2048]{1,0:T(8,128)} fusion(f32[256,512]{1,0:T(8,128)S(1)} %copy-done, f32[2048,512]{1,0:T(8,128)} %all-gather.2.cloned.1.call-done), kind=kOutput, calls=%fused_computation | convolution fusion | flops 3221225472 | bytes 6815744 | tf_op jit(solution)/shard_map/dot_general | solution.py:9
  66.0 0.0 reduce-scatter.2.cloned.1.call-update
  66.0 34.1 %reduce-scatter.2.cloned.1.call-done = f32[64,2048]{1,0:T(8,128)} async-done(((f32[256,2048]{1,0:T(8,128)}), f32[64,2048]{1,0:T(8,128)}) %reduce-scatter.2.cloned.1.call-update) | async-done | bytes 524304 | tf_op jit(solution)/shard_map/reduce_scatter | solution.py:16
Async XLA Ops:
  6.5 52.3 %copy-start = (f32[256,512]{1,0:T(8,128)S(1)}, f32[256,512]{1,0:T(8,128)}, u32[]{:S(2)}) copy-start(f32[256,512]{1,0:T(8,128)} %param.2) | copy-start | bytes 1572868
  6.5 52.3 %all-gather.2.cloned.1.call-start = ((), (), s32[]{:S(2)}) async-start(), calls=%async_computation.1 | async-start | bytes 4718592 | tf_op jit(solution)/shard_map/all_gather | solution.py:8
  7.3 92.8 %reduce-scatter.2.cloned.1.call-start = ((), (), s32[]{:S(2)}) async-start(), calls=%async_computation.2 | async-start | bytes 2621440 | tf_op jit(solution)/shard_map/reduce_scatter | solution.py:16
Sparse Core Ops, SparseCore 0:
  9.0 49.8 all-gather.1
  66.1 33.9 reduce-scatter.1
where the time goes:
time: 107 us
  waiting for transfers between devices  86.3 us (81%)
  between operations  13.4 us (13%)
  matrix products  7.14 us (7%)
    all_gather x1, waiting for transfers between devices, on_device(): panel = lax.all_gather(integrals, 'wide', axis=0, tiled=True)  51.5 us
    reduce_scatter x1, waiting for transfers between devices, on_device(): return lax.psum_scatter(part, 'col', scatter_dimension=0, tiled=True)  34.1 us
    dot_general x1, matrix products, on_device(): lax.dot_general(amplitudes, panel, (((1,), (1,)), ((), ())), precision=la...  7.14 us
  transfers between devices with their start and end apart: 2, of which 2 were waited for; matrix products, arithmetic and copies ran while one was open for 0% of the time, Pallas kernels for 0%

commit v1 on v0

--- a/solution.py
+++ b/solution.py
@@ -1,11 +1,37 @@
+import functools
 import jax
 import jax.numpy as jnp
 from jax import lax
 from jax.sharding import PartitionSpec as P
+from jax.lax import axis_index, axis_size, ppermute
+
+
+def load_yards(inp, dimension_no):
+    val2 = list(inp.shape[1:])
+    val2[dimension_no] *= inp.shape[0]
+    return jnp.moveaxis(inp, 0, dimension_no).reshape(val2)
+
+
+def carry_stacks_all_for(z_in, a_name, array_axis):
+    width = axis_size(a_name)
+    f_next = range(width)
+    far_arr = map(lambda b: (b, (b + 1) % width), f_next)
+    seen = list(far_arr)
+    rack = [z_in]
+    while len(rack) < width:
+        piece_out = ppermute(rack[-1], a_name, seen)
+        rack.append(piece_out)
+    lower = axis_index(a_name)
+    opened = jnp.stack(rack)
+    rack = opened[(lower - jnp.arange(width)) % width]
+    return load_yards(rack, array_axis)
+
+
+measure_the_rates = functools.partial(carry_stacks_all_for, a_name="wide", array_axis=0)
 
 
 def on_device(amplitudes, integrals):
-    panel = lax.all_gather(integrals, "wide", axis=0, tiled=True)
+    panel = measure_the_rates(integrals)
     part = lax.dot_general(
         amplitudes,
         panel,

time: 107 us -> 135 us (1.26)
  waiting for transfers between devices: 86.3 us -> 101 us
  local copies, waits for them, and re-layouts: 0.01 us -> 14.6 us
  matrix products: 7.14 us -> 5.28 us
    ppermute x0 -> x7, waiting for transfers between devices: none -> 66.6 us  [carry_stacks_all_for(): piece_out = ppermute(rack[-1], a_name, seen)]
    all_gather x1 -> x0, waiting for transfers between devices: 51.5 us -> none  [on_device(): panel = lax.all_gather(integrals, 'wide', axis=0, tiled=True)]
    unnamed x2 -> x10, local copies, waits for them, and re-layouts: 0.01 us -> 8.78 us
    gather x0 -> x1, local copies, waits for them, and re-layouts: none -> 4.98 us  [carry_stacks_all_for(): rack = opened[(lower - jnp.arange(width)) % width]]
    dot_general x1, matrix products: 7.14 us -> 5.28 us  [on_device(): lax.dot_general(amplitudes, panel, (((1,), (1,)), ((), ())), precision=la...]
  transfers between devices with their start and end apart: 2 -> 8, of which waited for: 2 -> 8; matrix products, arithmetic and copies ran while one was open for 0% -> 5% of each run, Pallas kernels for 0% -> 0%
where the time goes in v1:
time: 135 us; the launch traced here: 134 us
  waiting for transfers between devices  101 us (75%)
  local copies, waits for them, and re-layouts  14.6 us (11%)
  between operations  13.4 us (10%)
  matrix products  5.28 us (4%)
    ppermute x7, waiting for transfers between devices, carry_stacks_all_for(): piece_out = ppermute(rack[-1], a_name, seen)  66.6 us
    reduce_scatter x1, waiting for transfers between devices, on_device(): return lax.psum_scatter(part, 'col', scatter_dimension=0, tiled=True)  34 us
    unnamed x10, local copies, waits for them, and re-layouts  8.78 us
    dot_general x1, matrix products, on_device(): lax.dot_general(amplitudes, panel, (((1,), (1,)), ((), ())), precision=la...  5.28 us
    gather x1, local copies, waits for them, and re-layouts, carry_stacks_all_for(): rack = opened[(lower - jnp.arange(width)) % width]  4.98 us
  transfers between devices with their start and end apart: 8, of which 8 were waited for; matrix products, arithmetic and copies ran while one was open for 5% of the time, Pallas kernels for 0%

profile of v1, /device:TPU:0, one launch (start us, length us, event | category | flops | bytes accessed | tf_op | source)
XLA Modules:
  0.0 134.4 jit_solution(9763086837142303598)
XLA Ops:
  6.5 0.0 copy-start
  6.5 0.0 reduce-scatter.4.cloned.1.call-start
  6.5 0.5 collective-permute-start
  7.0 11.1 %collective-permute-done = f32[256,512]{1,0:T(8,128)S(1)} collective-permute-done((f32[256,512]{1,0:T(8,128)}, f32[256,512]{1,0:T(8,128)S(1)}, u32[]{:S(2)}, u32[]{:S(2)}) %collective-permute-start) | collective-permute-done | bytes 524320 | tf_op jit(solution)/shard_map/ppermute | solution.py:22
  18.1 0.0 collective-permute-start.1
  18.1 10.4 %collective-permute-done.1 = f32[256,512]{1,0:T(8,128)S(1)} collective-permute-done((f32[256,512]{1,0:T(8,128)S(1)}, f32[256,512]{1,0:T(8,128)S(1)}, u32[]{:S(2)}, u32[]{:S(2)}) %collective-permute-start.1) | collective-permute-done | bytes 524320 | tf_op jit(solution)/shard_map/ppermute | solution.py:22
  28.5 0.0 collective-permute-start.2
  28.5 10.4 %collective-permute-done.2 = f32[256,512]{1,0:T(8,128)S(1)} collective-permute-done((f32[256,512]{1,0:T(8,128)S(1)}, f32[256,512]{1,0:T(8,128)S(1)}, u32[]{:S(2)}, u32[]{:S(2)}) %collective-permute-start.2) | collective-permute-done | bytes 524320 | tf_op jit(solution)/shard_map/ppermute | solution.py:22
  38.9 0.0 collective-permute-start.3
  38.9 10.4 %collective-permute-done.3 = f32[256,512]{1,0:T(8,128)S(1)} collective-permute-done((f32[256,512]{1,0:T(8,128)S(1)}, f32[256,512]{1,0:T(8,128)S(1)}, u32[]{:S(2)}, u32[]{:S(2)}) %collective-permute-start.3) | collective-permute-done | bytes 524320 | tf_op jit(solution)/shard_map/ppermute | solution.py:22
  49.3 0.0 collective-permute-start.4
  49.3 1.9 %bitcast_dynamic-update-slice_fusion.7 = f32[8,256,512]{2,1,0:T(8,128)} fusion(f32[256,512]{1,0:T(8,128)} %param.3), kind=kLoop, calls=%fused_computation.9 | loop fusion | bytes 1048576
  51.2 8.5 %collective-permute-done.4 = f32[256,512]{1,0:T(8,128)S(1)} collective-permute-done((f32[256,512]{1,0:T(8,128)S(1)}, f32[256,512]{1,0:T(8,128)S(1)}, u32[]{:S(2)}, u32[]{:S(2)}) %collective-permute-start.4) | collective-permute-done | bytes 524320 | tf_op jit(solution)/shard_map/ppermute | solution.py:22
  59.7 0.0 collective-permute-start.5
  59.7 0.8 bitcast_dynamic-update-slice_fusion.6
  60.6 0.8 bitcast_dynamic-update-slice_fusion.5
  61.4 0.8 bitcast_dynamic-update-slice_fusion.4
  62.2 7.9 %collective-permute-done.5 = f32[256,512]{1,0:T(8,128)S(1)} collective-permute-done((f32[256,512]{1,0:T(8,128)S(1)}, f32[256,512]{1,0:T(8,128)S(1)}, u32[]{:S(2)}, u32[]{:S(2)}) %collective-permute-start.5) | collective-permute-done | bytes 524320 | tf_op jit(solution)/shard_map/ppermute | solution.py:22
  70.1 0.0 collective-permute-start.6
  70.1 0.8 bitcast_dynamic-update-slice_fusion.3
  71.0 0.8 bitcast_dynamic-update-slice_fusion.2
  71.8 0.8 bitcast_dynamic-update-slice_fusion.1
  72.7 7.9 %collective-permute-done.6 = f32[256,512]{1,0:T(8,128)S(1)} collective-permute-done((f32[256,512]{1,0:T(8,128)S(1)}, f32[256,512]{1,0:T(8,128)S(1)}, u32[]{:S(2)}, u32[]{:S(2)}) %collective-permute-start.6) | collective-permute-done | bytes 524320 | tf_op jit(solution)/shard_map/ppermute | solution.py:22
  80.5 0.8 bitcast_dynamic-update-slice_fusion
  81.4 5.0 %gather_fusion = f32[8,256,512]{2,1,0:T(8,128)} fusion(f32[8,256,512]{2,1,0:T(8,128)} %bitcast_dynamic-update-slice_fusion, s32[1024]{0:T(1024)S(1)} %pad_clamp_fusion), kind=kCustom, calls=%fused_computation | custom fusion | bytes 8388640 | tf_op jit(solution)/shard_map/gather | solution.py:26
  86.3 0.0 copy-done
  86.3 5.3 %convolution_bitcast_fusion = f32[256,2048]{0,1:T(8,128)S(1)} fusion(f32[2048,512]{1,0:T(8,128)} %bitcast.24, f32[256,512]{1,0:T(8,128)S(1)} %copy-done), kind=kOutput, calls=%fused_computation.1 | convolution fusion | flops 3221225472 | bytes 6815744 | tf_op jit(solution)/shard_map/dot_general | solution.py:35
  91.6 1.9 %copy.5 = f32[256,2048]{1,0:T(8,128)} copy(f32[256,2048]{0,1:T(8,128)S(1)} %convolution_bitcast_fusion) | data formatting | bytes 4194304
  93.5 0.0 reduce-scatter.4.cloned.1.call-update
  93.5 34.0 %reduce-scatter.4.cloned.1.call-done = f32[64,2048]{1,0:T(8,128)} async-done(((f32[256,2048]{1,0:T(8,128)}), f32[64,2048]{1,0:T(8,128)}) %reduce-scatter.4.cloned.1.call-update) | async-done | bytes 524304 | tf_op jit(solution)/shard_map/reduce_scatter | solution.py:42
  (2 shorter events, 0.0 us)
Async XLA Ops:
  6.5 79.8 %copy-start = (f32[256,512]{1,0:T(8,128)S(1)}, f32[256,512]{1,0:T(8,128)}, u32[]{:S(2)}) copy-start(f32[256,512]{1,0:T(8,128)} %param.2) | copy-start | bytes 1572868
  6.5 121.0 %reduce-scatter.4.cloned.1.call-start = ((), (), s32[]{:S(2)}) async-start(), calls=%async_computation.1 | async-start | bytes 2621440 | tf_op jit(solution)/shard_map/reduce_scatter | solution.py:42
  6.5 11.6 %collective-permute-start = (f32[256,512]{1,0:T(8,128)}, f32[256,512]{1,0:T(8,128)S(1)}, u32[]{:S(2)}, u32[]{:S(2)}) collective-permute-start(f32[256,512]{1,0:T(8,128)} %param.3), channel_id=1, source_target_pairs={{0,4},{4,8},{8,12},{12,16},{16,20},{20,24},{24,28},{28,0},{1,5},{5... | collective-permute-start | bytes 1572872 | tf_op jit(solution)/shard_map/ppermute | solution.py:22
  18.1 10.4 %collective-permute-start.1 = (f32[256,512]{1,0:T(8,128)S(1)}, f32[256,512]{1,0:T(8,128)S(1)}, u32[]{:S(2)}, u32[]{:S(2)}) collective-permute-start(f32[256,512]{1,0:T(8,128)S(1)} %collective-permute-done), channel_id=1, source_target_pairs={{0,4},{4,8},{8,12},{12,16},{16,20},{20,24},{24,28},{28,0},{1,5},{5... | collective-permute-start | bytes 1572872 | tf_op jit(solution)/shard_map/ppermute | solution.py:22
  28.5 10.4 %collective-permute-start.2 = (f32[256,512]{1,0:T(8,128)S(1)}, f32[256,512]{1,0:T(8,128)S(1)}, u32[]{:S(2)}, u32[]{:S(2)}) collective-permute-start(f32[256,512]{1,0:T(8,128)S(1)} %collective-permute-done.1), channel_id=1, source_target_pairs={{0,4},{4,8},{8,12},{12,16},{16,20},{20,24},{24,28},{28,0},{1,5},{5... | collective-permute-start | bytes 1572872 | tf_op jit(solution)/shard_map/ppermute | solution.py:22
  38.9 10.4 %collective-permute-start.3 = (f32[256,512]{1,0:T(8,128)S(1)}, f32[256,512]{1,0:T(8,128)S(1)}, u32[]{:S(2)}, u32[]{:S(2)}) collective-permute-start(f32[256,512]{1,0:T(8,128)S(1)} %collective-permute-done.2), channel_id=1, source_target_pairs={{0,4},{4,8},{8,12},{12,16},{16,20},{20,24},{24,28},{28,0},{1,5},{5... | collective-permute-start | bytes 1572872 | tf_op jit(solution)/shard_map/ppermute | solution.py:22
  49.3 10.4 %collective-permute-start.4 = (f32[256,512]{1,0:T(8,128)S(1)}, f32[256,512]{1,0:T(8,128)S(1)}, u32[]{:S(2)}, u32[]{:S(2)}) collective-permute-start(f32[256,512]{1,0:T(8,128)S(1)} %collective-permute-done.3), channel_id=1, source_target_pairs={{0,4},{4,8},{8,12},{12,16},{16,20},{20,24},{24,28},{28,0},{1,5},{5... | collective-permute-start | bytes 1572872 | tf_op jit(solution)/shard_map/ppermute | solution.py:22
  59.7 10.4 %collective-permute-start.5 = (f32[256,512]{1,0:T(8,128)S(1)}, f32[256,512]{1,0:T(8,128)S(1)}, u32[]{:S(2)}, u32[]{:S(2)}) collective-permute-start(f32[256,512]{1,0:T(8,128)S(1)} %collective-permute-done.4), channel_id=1, source_target_pairs={{0,4},{4,8},{8,12},{12,16},{16,20},{20,24},{24,28},{28,0},{1,5},{5... | collective-permute-start | bytes 1572872 | tf_op jit(solution)/shard_map/ppermute | solution.py:22
  70.1 10.4 %collective-permute-start.6 = (f32[256,512]{1,0:T(8,128)S(1)}, f32[256,512]{1,0:T(8,128)S(1)}, u32[]{:S(2)}, u32[]{:S(2)}) collective-permute-start(f32[256,512]{1,0:T(8,128)S(1)} %collective-permute-done.5), channel_id=1, source_target_pairs={{0,4},{4,8},{8,12},{12,16},{16,20},{20,24},{24,28},{28,0},{1,5},{5... | collective-permute-start | bytes 1572872 | tf_op jit(solution)/shard_map/ppermute | solution.py:22
Sparse Core Ops, SparseCore 0:
  93.6 33.8 reduce-scatter.3
